TPU v7x, 32 devices: a whole 2x2x4 slice. The times are simulated.
32 devices in a mesh: depth: 8 (over y, x, core), dp: 4 (over z).
Axes of the slice: x: 2, y: 2, z: 4, core: 2. Of those that a mesh axis runs over, the one named last changes fastest.
Arguments:
- token_ids: int32 [512], P('dp'), may hold values from 0 to 10239
- embedding: bfloat16 [10240, 512], P('depth'), may hold values from -6 to 6
- w_up: bfloat16 [16, 512, 2048], P('depth'), may hold values from -0.25 to 0.25
- w_down: bfloat16 [16, 2048, 512], P('depth'), may hold values from -0.125 to 0.125
- cotangent: bfloat16 [512, 512], P('dp'), may hold values from -0.119628906 to 0.119628906
Outputs:
- grad_up: float32 [16, 512, 2048], P('depth', 'dp')
- grad_down: float32 [16, 2048, 512], P('depth', 'dp')
All inputs are finite; a program needn't handle non-finite values.
Results may differ from a plain program's by a relative error of at most 0.03.
Values may be sent and summed in bfloat16 or wider, within the bound.
No kernel may reach another device: no remote copies, remote signals or barrier semaphores. Data moves between devices by JAX's collectives and lax.ppermute only.
A program may use at most 64 MiB of HBM per device.

v0:
```python
import jax
import jax.numpy as jnp
from jax import lax
from jax.sharding import PartitionSpec as P

RELAX = 3
EPSILON = 1e-06
GAMMA = 0.05


def shifted(block, axis, distance):
    devices = range(lax.axis_size(axis))
    route = [(i - distance, i) for i in devices if i - distance in devices]
    return lax.ppermute(block, axis, route)


def layer_forward(state, weight_up, weight_down):
    scale = lax.rsqrt(jnp.mean(state * state, axis=-1, keepdims=True) + EPSILON)
    normed = (state * scale).astype(jnp.bfloat16)
    before = jnp.dot(normed, weight_up, preferred_element_type=jnp.float32)
    hidden = jax.nn.silu(before).astype(jnp.bfloat16)
    output = state + jnp.dot(hidden, weight_down, preferred_element_type=jnp.float32)
    return (output, (scale, normed, before, hidden))


def layer_adjoint(state, saved, adjoint, weight_up, weight_down):
    scale, normed, before, hidden = saved
    adjoint_low = adjoint.astype(jnp.bfloat16)
    toward_hidden = lax.dot_general(
        adjoint_low, weight_down, (((1,), (1,)), ((), ())), preferred_element_type=jnp.float32
    )
    sigma = jax.nn.sigmoid(before)
    delta = (toward_hidden * sigma * (1.0 + before * (1.0 - sigma))).astype(jnp.bfloat16)
    toward_normed = lax.dot_general(
        delta, weight_up, (((1,), (1,)), ((), ())), preferred_element_type=jnp.float32
    )
    unit = state * scale
    inner = jnp.mean(toward_normed * unit, axis=-1, keepdims=True)
    return (adjoint + scale * (toward_normed - unit * inner), adjoint_low, delta)


def coarse_matrix(weight_up, weight_down):
    total = jnp.dot(weight_up[0], weight_down[0], preferred_element_type=jnp.float32)
    total = total + jnp.dot(weight_up[1], weight_down[1], preferred_element_type=jnp.float32)
    return jnp.eye(weight_up.shape[1], dtype=jnp.float32) + GAMMA * total


def shards(token_ids, embedding, w_up, w_down, cotangent):
    depth = lax.axis_size("depth")
    position = lax.axis_index("depth")
    first = position == 0
    final_block = position == depth - 1
    layers = w_up.shape[0]
    vocab_rows = embedding.shape[0]
    local_ids = token_ids - position * vocab_rows
    inside = (local_ids >= 0) & (local_ids < vocab_rows)
    picked = jnp.take(embedding, jnp.clip(local_ids, 0, vocab_rows - 1), axis=0)
    picked = jnp.where(inside[:, None], picked, jnp.zeros_like(picked)).astype(jnp.float32)
    start = lax.psum(picked.astype(jnp.bfloat16), "depth").astype(jnp.float32)
    matrix = coarse_matrix(w_up, w_down)
    transposed = matrix.T
    zeros = jnp.zeros_like(start)
    coarse = start
    arrived_projection = zeros
    for sweep in range(RELAX):
        run_state = coarse
        for run_layer in range(layers):
            run_state, unused = layer_forward(run_state, w_up[run_layer], w_down[run_layer])
        projection = jnp.dot(coarse, matrix, precision=lax.Precision.HIGHEST)
        arrived, arrived_projection = shifted((run_state, projection), "depth", 1)
        coarse = jnp.where(first, start, arrived)
    tau = coarse - arrived_projection

    def forward_turn(turn, incoming):
        carried = jnp.dot(incoming + tau, matrix, precision=lax.Precision.HIGHEST)
        return shifted(carried.astype(jnp.bfloat16), "depth", 1).astype(carried.dtype)

    incoming = lax.fori_loop(0, depth - 1, forward_turn, zeros)
    corrected = incoming + tau
    states = []
    saves = []
    state = corrected
    for layer in range(layers):
        states.append(state)
        state, saved = layer_forward(state, w_up[layer], w_down[layer])
        saves.append(saved)

    def run_adjoint(adjoint):
        for layer in reversed(range(layers)):
            adjoint, low, delta = layer_adjoint(
                states[layer], saves[layer], adjoint, w_up[layer], w_down[layer]
            )
        return adjoint

    final = cotangent.astype(jnp.float32)
    adjoint_state = final
    back_projection = zeros
    for sweep in range(RELAX):
        begun = run_adjoint(adjoint_state)
        projection = jnp.dot(adjoint_state, transposed, precision=lax.Precision.HIGHEST)
        arrived, back_projection = (
            shifted(begun.astype(jnp.bfloat16), "depth", -1).astype(begun.dtype),
            shifted(projection.astype(jnp.bfloat16), "depth", -1).astype(projection.dtype),
        )
        adjoint_state = jnp.where(final_block, final, arrived)
    back_tau = adjoint_state - back_projection

    def backward_turn(turn, incoming):
        carried = jnp.dot(incoming + back_tau, transposed, precision=lax.Precision.HIGHEST)
        return shifted(carried.astype(jnp.bfloat16), "depth", -1).astype(carried.dtype)

    back_incoming = lax.fori_loop(0, depth - 1, backward_turn, zeros)
    adjoint = back_incoming + back_tau
    lows = [None] * layers
    deltas = [None] * layers
    for layer in reversed(range(layers)):
        adjoint, low, delta = layer_adjoint(
            states[layer], saves[layer], adjoint, w_up[layer], w_down[layer]
        )
        lows[layer] = low
        deltas[layer] = delta
    normed_all = jnp.stack([saves[layer][1] for layer in range(layers)], 0)
    hidden_all = jnp.stack([saves[layer][3] for layer in range(layers)], 0)
    delta_all = jnp.stack(deltas, 0)
    low_all = jnp.stack(lows, 0)
    normed_part, hidden_part = (
        lax.all_to_all(normed_all, "dp", split_axis=2, concat_axis=1, tiled=True),
        lax.all_to_all(hidden_all, "dp", split_axis=2, concat_axis=1, tiled=True),
    )
    delta_whole, low_whole = (
        lax.all_gather(delta_all, "dp", axis=1, tiled=True),
        lax.all_gather(low_all, "dp", axis=1, tiled=True),
    )
    grad_up = jnp.einsum(
        "ltd,ltf->ldf", normed_part, delta_whole, preferred_element_type=jnp.float32
    )
    grad_down = jnp.einsum(
        "ltf,ltd->lfd", hidden_part, low_whole, preferred_element_type=jnp.float32
    )
    return (grad_up, grad_down)


def solution(mesh):
    in_specs = (
        P("dp"),
        P("depth", None),
        P("depth", None, None),
        P("depth", None, None),
        P("dp", None),
    )
    out_specs = (P("depth", "dp", None), P("depth", "dp", None))
    return jax.shard_map(shards, mesh=mesh, in_specs=in_specs, out_specs=out_specs, check_vma=False)
```

profile of v0, /device:TPU:0, one launch (start us, length us, event | category | flops | bytes accessed | tf_op | source)
XLA Modules:
  0.0 437.5 jit_solution(14068713169038172877)
XLA Ops:
  10.2 57.6 %all-reduce.2.cloned.1.call-done = bf16[128,512]{1,0:T(8,128)(2,1)} async-done(((bf16[128,512]{1,0:T(8,128)(2,1)}), bf16[128,512]{1,0:T(8,128)(2,1)}) %all-reduce.2.cloned.1.call-update) | async-done | bytes 131088 | tf_op jit(solution)/shard_map/psum | solution.py:59
  109.1 4.5 %collective-permute-start.5 = (f32[128,512]{1,0:T(8,128)}, f32[128,512]{1,0:T(8,128)S(1)}, u32[]{:S(2)}, u32[]{:S(2)}) collective-permute-start(f32[128,512]{1,0:T(8,128)} %fusion.244), channel_id=1, source_target_pairs={{0,4},{4,8},{8,12},{12,16},{16,20},{20,24},{24,28},{1,5},{5,9},{9,... | collective-permute-start | bytes 786440 | tf_op jit(solution)/shard_map/ppermute | solution.py:14
  114.8 50.3 %while.22 = (s32[]{:T(128)}, f32[128,512]{1,0:T(8,128)S(1)}, f32[128,512]{1,0:T(8,128)S(1)}, f32[512,512]{1,0:T(8,128)S(1)}, s32[]{:T(128)}, /*index=5*/s32[]{:T(128)}) while((s32[]{:T(128)}, f32[128,512]{1,0:T(8,128)S(1)}, f32[128,512]{1,0:T(8,128)S(1)}, f32[512,512]{1,0:T(8,128)S(1)}, s32[]{:T(128)}, /*index=5*/s32[]{:T(128)}) %tuple.64), condition=%wide.region_8.9_spmd.clone, body=%wide.region_7.8_spmd.clone.sunk | while | flops 402915328 | bytes 2621559 | solution.py:78
  115.6 5.4 %collective-permute-start = (bf16[128,512]{1,0:T(8,128)(2,1)S(1)}, bf16[128,512]{1,0:T(8,128)(2,1)S(1)}, u32[]{:S(2)}, u32[]{:S(2)}) collective-permute-start(bf16[128,512]{1,0:T(8,128)(2,1)S(1)} %convolution_convert_fusion.5), channel_id=1, source_target_pairs={{0,4},{4,8},{8,12},{12,16},{16,20},{20,24},{24,28},{1,5},{5,9},{9,... | collective-permute-start | bytes 393224 | tf_op jit(solution)/shard_map/while/body/eval_jaxpr/ppermute | solution.py:14
  122.8 5.2 %collective-permute-start = (bf16[128,512]{1,0:T(8,128)(2,1)S(1)}, bf16[128,512]{1,0:T(8,128)(2,1)S(1)}, u32[]{:S(2)}, u32[]{:S(2)}) collective-permute-start(bf16[128,512]{1,0:T(8,128)(2,1)S(1)} %convolution_convert_fusion.5), channel_id=1, source_target_pairs={{0,4},{4,8},{8,12},{12,16},{16,20},{20,24},{24,28},{1,5},{5,9},{9,... | collective-permute-start | bytes 393224 | tf_op jit(solution)/shard_map/while/body/eval_jaxpr/ppermute | solution.py:14
  129.8 5.3 %collective-permute-start = (bf16[128,512]{1,0:T(8,128)(2,1)S(1)}, bf16[128,512]{1,0:T(8,128)(2,1)S(1)}, u32[]{:S(2)}, u32[]{:S(2)}) collective-permute-start(bf16[128,512]{1,0:T(8,128)(2,1)S(1)} %convolution_convert_fusion.5), channel_id=1, source_target_pairs={{0,4},{4,8},{8,12},{12,16},{16,20},{20,24},{24,28},{1,5},{5,9},{9,... | collective-permute-start | bytes 393224 | tf_op jit(solution)/shard_map/while/body/eval_jaxpr/ppermute | solution.py:14
  136.8 5.3 %collective-permute-start = (bf16[128,512]{1,0:T(8,128)(2,1)S(1)}, bf16[128,512]{1,0:T(8,128)(2,1)S(1)}, u32[]{:S(2)}, u32[]{:S(2)}) collective-permute-start(bf16[128,512]{1,0:T(8,128)(2,1)S(1)} %convolution_convert_fusion.5), channel_id=1, source_target_pairs={{0,4},{4,8},{8,12},{12,16},{16,20},{20,24},{24,28},{1,5},{5,9},{9,... | collective-permute-start | bytes 393224 | tf_op jit(solution)/shard_map/while/body/eval_jaxpr/ppermute | solution.py:14
  143.9 5.3 %collective-permute-start = (bf16[128,512]{1,0:T(8,128)(2,1)S(1)}, bf16[128,512]{1,0:T(8,128)(2,1)S(1)}, u32[]{:S(2)}, u32[]{:S(2)}) collective-permute-start(bf16[128,512]{1,0:T(8,128)(2,1)S(1)} %convolution_convert_fusion.5), channel_id=1, source_target_pairs={{0,4},{4,8},{8,12},{12,16},{16,20},{20,24},{24,28},{1,5},{5,9},{9,... | collective-permute-start | bytes 393224 | tf_op jit(solution)/shard_map/while/body/eval_jaxpr/ppermute | solution.py:14
  151.0 5.3 %collective-permute-start = (bf16[128,512]{1,0:T(8,128)(2,1)S(1)}, bf16[128,512]{1,0:T(8,128)(2,1)S(1)}, u32[]{:S(2)}, u32[]{:S(2)}) collective-permute-start(bf16[128,512]{1,0:T(8,128)(2,1)S(1)} %convolution_convert_fusion.5), channel_id=1, source_target_pairs={{0,4},{4,8},{8,12},{12,16},{16,20},{20,24},{24,28},{1,5},{5,9},{9,... | collective-permute-start | bytes 393224 | tf_op jit(solution)/shard_map/while/body/eval_jaxpr/ppermute | solution.py:14
  158.1 6.1 %collective-permute-start = (bf16[128,512]{1,0:T(8,128)(2,1)S(1)}, bf16[128,512]{1,0:T(8,128)(2,1)S(1)}, u32[]{:S(2)}, u32[]{:S(2)}) collective-permute-start(bf16[128,512]{1,0:T(8,128)(2,1)S(1)} %convolution_convert_fusion.5), channel_id=1, source_target_pairs={{0,4},{4,8},{8,12},{12,16},{16,20},{20,24},{24,28},{1,5},{5,9},{9,... | collective-permute-start | bytes 393224 | tf_op jit(solution)/shard_map/while/body/eval_jaxpr/ppermute | solution.py:14
  181.6 5.7 %collective-permute-done.6 = bf16[128,512]{1,0:T(8,128)(2,1)S(1)} collective-permute-done((bf16[128,512]{1,0:T(8,128)(2,1)S(1)}, bf16[128,512]{1,0:T(8,128)(2,1)S(1)}, u32[]{:S(2)}, u32[]{:S(2)}) %collective-permute-start.6) | collective-permute-done | bytes 131104 | tf_op jit(solution)/shard_map/ppermute | solution.py:14
  197.4 6.6 %collective-permute-done.7 = bf16[128,512]{1,0:T(8,128)(2,1)S(1)} collective-permute-done((bf16[128,512]{1,0:T(8,128)(2,1)S(1)}, bf16[128,512]{1,0:T(8,128)(2,1)S(1)}, u32[]{:S(2)}, u32[]{:S(2)}) %collective-permute-start.7) | collective-permute-done | bytes 131104 | tf_op jit(solution)/shard_map/ppermute | solution.py:14
  207.1 4.8 %multiply_reduce_fusion.2 = (f32[128]{0:T(128)S(1)}, f32[128,512]{1,0:T(8,128)}) fusion(f32[128,512]{1,0:T(8,128)S(1)} %get-tuple-element.122, f32[128]{0:T(128)S(1)} %add_rsqrt_fusion, bf16[2,512,2048]{2,1,0:T(8,128)(2,1)} %param.11, f32[128,2048]{1,0:T(8,128)} %fusion.43, bf16[2,2048,512]{2,1,0:T(8,128)(2,1)} %param.12, ...), kind=kOutput, calls=%fused_computation.173 | convolution fusion | flops 539688832 | bytes 6030337 | tf_op jit(solution)/shard_map/dot_general | solution.py:34
  226.9 56.5 %while.23 = (s32[]{:T(128)}, f32[128,512]{1,0:T(8,128)S(1)}, f32[128,512]{1,0:T(8,128)S(1)}, f32[512,512]{1,0:T(8,128)S(1)}, s32[]{:T(128)}, /*index=5*/s32[]{:T(128)}) while((s32[]{:T(128)}, f32[128,512]{1,0:T(8,128)S(1)}, f32[128,512]{1,0:T(8,128)S(1)}, f32[512,512]{1,0:T(8,128)S(1)}, s32[]{:T(128)}, ...), condition=%wide.region_18.19_spmd.clone, body=%wide.region_17.18_spmd.clone.sunk | while | flops 402915328 | bytes 2621559 | solution.py:112
  228.9 6.6 %collective-permute-done.1 = bf16[128,512]{1,0:T(8,128)(2,1)S(1)} collective-permute-done((bf16[128,512]{1,0:T(8,128)(2,1)S(1)}, bf16[128,512]{1,0:T(8,128)(2,1)S(1)}, u32[]{:S(2)}, u32[]{:S(2)}) %collective-permute-start.1) | collective-permute-done | bytes 131104 | tf_op jit(solution)/shard_map/while/body/eval_jaxpr/ppermute | solution.py:14
  237.6 5.9 %collective-permute-done.1 = bf16[128,512]{1,0:T(8,128)(2,1)S(1)} collective-permute-done((bf16[128,512]{1,0:T(8,128)(2,1)S(1)}, bf16[128,512]{1,0:T(8,128)(2,1)S(1)}, u32[]{:S(2)}, u32[]{:S(2)}) %collective-permute-start.1) | collective-permute-done | bytes 131104 | tf_op jit(solution)/shard_map/while/body/eval_jaxpr/ppermute | solution.py:14
  245.6 5.9 %collective-permute-done.1 = bf16[128,512]{1,0:T(8,128)(2,1)S(1)} collective-permute-done((bf16[128,512]{1,0:T(8,128)(2,1)S(1)}, bf16[128,512]{1,0:T(8,128)(2,1)S(1)}, u32[]{:S(2)}, u32[]{:S(2)}) %collective-permute-start.1) | collective-permute-done | bytes 131104 | tf_op jit(solution)/shard_map/while/body/eval_jaxpr/ppermute | solution.py:14
  253.5 5.9 %collective-permute-done.1 = bf16[128,512]{1,0:T(8,128)(2,1)S(1)} collective-permute-done((bf16[128,512]{1,0:T(8,128)(2,1)S(1)}, bf16[128,512]{1,0:T(8,128)(2,1)S(1)}, u32[]{:S(2)}, u32[]{:S(2)}) %collective-permute-start.1) | collective-permute-done | bytes 131104 | tf_op jit(solution)/shard_map/while/body/eval_jaxpr/ppermute | solution.py:14
  261.5 5.9 %collective-permute-done.1 = bf16[128,512]{1,0:T(8,128)(2,1)S(1)} collective-permute-done((bf16[128,512]{1,0:T(8,128)(2,1)S(1)}, bf16[128,512]{1,0:T(8,128)(2,1)S(1)}, u32[]{:S(2)}, u32[]{:S(2)}) %collective-permute-start.1) | collective-permute-done | bytes 131104 | tf_op jit(solution)/shard_map/while/body/eval_jaxpr/ppermute | solution.py:14
  269.5 5.9 %collective-permute-done.1 = bf16[128,512]{1,0:T(8,128)(2,1)S(1)} collective-permute-done((bf16[128,512]{1,0:T(8,128)(2,1)S(1)}, bf16[128,512]{1,0:T(8,128)(2,1)S(1)}, u32[]{:S(2)}, u32[]{:S(2)}) %collective-permute-start.1) | collective-permute-done | bytes 131104 | tf_op jit(solution)/shard_map/while/body/eval_jaxpr/ppermute | solution.py:14
  277.4 5.9 %collective-permute-done.1 = bf16[128,512]{1,0:T(8,128)(2,1)S(1)} collective-permute-done((bf16[128,512]{1,0:T(8,128)(2,1)S(1)}, bf16[128,512]{1,0:T(8,128)(2,1)S(1)}, u32[]{:S(2)}, u32[]{:S(2)}) %collective-permute-start.1) | collective-permute-done | bytes 131104 | tf_op jit(solution)/shard_map/while/body/eval_jaxpr/ppermute | solution.py:14
  296.1 4.6 %all-to-all-start = ((bf16[2,128,512]{1,0,2:T(2,128)(2,1)}), bf16[2,128,512]{1,0,2:T(2,128)(2,1)}, u32[]{:S(2)}, u32[]{:S(2)}) async-start(bf16[2,128,512]{1,0,2:T(2,128)(2,1)} %copy.10), calls=%async_computation | async-start | bytes 524288 | tf_op jit(solution)/shard_map/all_to_all | solution.py:127
  313.1 37.0 %all-to-all-done.1 = bf16[2,128,2048]{1,0,2:T(2,128)(2,1)S(1)} async-done(((bf16[2,128,2048]{1,0,2:T(2,128)(2,1)}), bf16[2,128,2048]{1,0,2:T(2,128)(2,1)S(1)}, u32[]{:S(2)}, u32[]{:S(2)}) %all-to-all-start.1) | async-done | bytes 1048608 | tf_op jit(solution)/shard_map/all_to_all | solution.py:128
  354.8 72.0 %all-gather.3.cloned.1.call-done = bf16[2,512,2048]{2,1,0:T(8,128)(2,1)} async-done(((bf16[2,128,2048]{2,1,0:T(8,128)(2,1)}), bf16[2,512,2048]{2,1,0:T(8,128)(2,1)}) %all-gather.3.cloned.1.call-update) | async-done | bytes 4194320 | tf_op jit(solution)/shard_map/all_gather | solution.py:131
  (166 shorter events, 150.0 us)
Async XLA Ops:
  7.2 60.6 %all-reduce.2.cloned.1.call-start = ((), (), s32[]{:S(2)}) async-start(), calls=%async_computation.2 | async-start | bytes 262144 | tf_op jit(solution)/shard_map/psum | solution.py:59
  10.1 341.2 %all-gather.5.cloned.1.call-start = ((), (), s32[]{:S(2)}) async-start(), calls=%async_computation.4 | async-start | bytes 1310720 | tf_op jit(solution)/shard_map/all_gather | solution.py:132
  87.8 7.2 %collective-permute-start.3 = (f32[128,512]{1,0:T(8,128)}, f32[128,512]{1,0:T(8,128)S(1)}, u32[]{:S(2)}, u32[]{:S(2)}) collective-permute-start(f32[128,512]{1,0:T(8,128)} %fusion.118), channel_id=1, source_target_pairs={{0,4},{4,8},{8,12},{12,16},{16,20},{20,24},{24,28},{1,5},{5,9},{9,... | collective-permute-start | bytes 786440 | tf_op jit(solution)/shard_map/ppermute | solution.py:14
  103.6 10.0 %collective-permute-start.4 = (f32[128,512]{1,0:T(8,128)}, f32[128,512]{1,0:T(8,128)}, u32[]{:S(2)}, u32[]{:S(2)}) collective-permute-start(f32[128,512]{1,0:T(8,128)} %fusion.121), channel_id=1, source_target_pairs={{0,4},{4,8},{8,12},{12,16},{16,20},{20,24},{24,28},{1,5},{5,9},{9,... | collective-permute-start | bytes 786440 | tf_op jit(solution)/shard_map/ppermute | solution.py:14
  115.6 6.4 %collective-permute-start = (bf16[128,512]{1,0:T(8,128)(2,1)S(1)}, bf16[128,512]{1,0:T(8,128)(2,1)S(1)}, u32[]{:S(2)}, u32[]{:S(2)}) collective-permute-start(bf16[128,512]{1,0:T(8,128)(2,1)S(1)} %convolution_convert_fusion.5), channel_id=1, source_target_pairs={{0,4},{4,8},{8,12},{12,16},{16,20},{20,24},{24,28},{1,5},{5,9},{9,... | collective-permute-start | bytes 393224 | tf_op jit(solution)/shard_map/while/body/eval_jaxpr/ppermute | solution.py:14
  129.8 6.3 %collective-permute-start = (bf16[128,512]{1,0:T(8,128)(2,1)S(1)}, bf16[128,512]{1,0:T(8,128)(2,1)S(1)}, u32[]{:S(2)}, u32[]{:S(2)}) collective-permute-start(bf16[128,512]{1,0:T(8,128)(2,1)S(1)} %convolution_convert_fusion.5), channel_id=1, source_target_pairs={{0,4},{4,8},{8,12},{12,16},{16,20},{20,24},{24,28},{1,5},{5,9},{9,... | collective-permute-start | bytes 393224 | tf_op jit(solution)/shard_map/while/body/eval_jaxpr/ppermute | solution.py:14
  136.8 6.3 %collective-permute-start = (bf16[128,512]{1,0:T(8,128)(2,1)S(1)}, bf16[128,512]{1,0:T(8,128)(2,1)S(1)}, u32[]{:S(2)}, u32[]{:S(2)}) collective-permute-start(bf16[128,512]{1,0:T(8,128)(2,1)S(1)} %convolution_convert_fusion.5), channel_id=1, source_target_pairs={{0,4},{4,8},{8,12},{12,16},{16,20},{20,24},{24,28},{1,5},{5,9},{9,... | collective-permute-start | bytes 393224 | tf_op jit(solution)/shard_map/while/body/eval_jaxpr/ppermute | solution.py:14
  143.9 6.3 %collective-permute-start = (bf16[128,512]{1,0:T(8,128)(2,1)S(1)}, bf16[128,512]{1,0:T(8,128)(2,1)S(1)}, u32[]{:S(2)}, u32[]{:S(2)}) collective-permute-start(bf16[128,512]{1,0:T(8,128)(2,1)S(1)} %convolution_convert_fusion.5), channel_id=1, source_target_pairs={{0,4},{4,8},{8,12},{12,16},{16,20},{20,24},{24,28},{1,5},{5,9},{9,... | collective-permute-start | bytes 393224 | tf_op jit(solution)/shard_map/while/body/eval_jaxpr/ppermute | solution.py:14
  151.0 6.3 %collective-permute-start = (bf16[128,512]{1,0:T(8,128)(2,1)S(1)}, bf16[128,512]{1,0:T(8,128)(2,1)S(1)}, u32[]{:S(2)}, u32[]{:S(2)}) collective-permute-start(bf16[128,512]{1,0:T(8,128)(2,1)S(1)} %convolution_convert_fusion.5), channel_id=1, source_target_pairs={{0,4},{4,8},{8,12},{12,16},{16,20},{20,24},{24,28},{1,5},{5,9},{9,... | collective-permute-start | bytes 393224 | tf_op jit(solution)/shard_map/while/body/eval_jaxpr/ppermute | solution.py:14
  158.1 7.1 %collective-permute-start = (bf16[128,512]{1,0:T(8,128)(2,1)S(1)}, bf16[128,512]{1,0:T(8,128)(2,1)S(1)}, u32[]{:S(2)}, u32[]{:S(2)}) collective-permute-start(bf16[128,512]{1,0:T(8,128)(2,1)S(1)} %convolution_convert_fusion.5), channel_id=1, source_target_pairs={{0,4},{4,8},{8,12},{12,16},{16,20},{20,24},{24,28},{1,5},{5,9},{9,... | collective-permute-start | bytes 393224 | tf_op jit(solution)/shard_map/while/body/eval_jaxpr/ppermute | solution.py:14
  180.3 7.0 %collective-permute-start.6 = (bf16[128,512]{1,0:T(8,128)(2,1)S(1)}, bf16[128,512]{1,0:T(8,128)(2,1)S(1)}, u32[]{:S(2)}, u32[]{:S(2)}) collective-permute-start(bf16[128,512]{1,0:T(8,128)(2,1)S(1)} %add_convert_fusion.3), channel_id=1, source_target_pairs={{4,0},{8,4},{12,8},{16,12},{20,16},{24,20},{28,24},{5,1},{9,5},{13... | collective-permute-start | bytes 393224 | tf_op jit(solution)/shard_map/ppermute | solution.py:14
  196.1 7.9 %collective-permute-start.7 = (bf16[128,512]{1,0:T(8,128)(2,1)S(1)}, bf16[128,512]{1,0:T(8,128)(2,1)S(1)}, u32[]{:S(2)}, u32[]{:S(2)}) collective-permute-start(bf16[128,512]{1,0:T(8,128)(2,1)S(1)} %add_convert_fusion.2), channel_id=1, source_target_pairs={{4,0},{8,4},{12,8},{16,12},{20,16},{24,20},{28,24},{5,1},{9,5},{13... | collective-permute-start | bytes 393224 | tf_op jit(solution)/shard_map/ppermute | solution.py:14
  205.8 16.4 %collective-permute-start.9 = (bf16[128,512]{1,0:T(8,128)(2,1)}, bf16[128,512]{1,0:T(8,128)(2,1)}, u32[]{:S(2)}, u32[]{:S(2)}) collective-permute-start(bf16[128,512]{1,0:T(8,128)(2,1)} %convolution_convert_fusion.2), channel_id=1, source_target_pairs={{4,0},{8,4},{12,8},{16,12},{20,16},{24,20},{28,24},{5,1},{9,5},{13... | collective-permute-start | bytes 393224 | tf_op jit(solution)/shard_map/ppermute | solution.py:14
  218.0 7.9 %collective-permute-start.8 = (bf16[128,512]{1,0:T(8,128)(2,1)}, bf16[128,512]{1,0:T(8,128)(2,1)S(1)}, u32[]{:S(2)}, u32[]{:S(2)}) collective-permute-start(bf16[128,512]{1,0:T(8,128)(2,1)} %get-tuple-element.110), channel_id=1, source_target_pairs={{4,0},{8,4},{12,8},{16,12},{20,16},{24,20},{28,24},{5,1},{9,5},{13... | collective-permute-start | bytes 393224 | tf_op jit(solution)/shard_map/ppermute | solution.py:14
  227.6 7.9 %collective-permute-start.1 = (bf16[128,512]{1,0:T(8,128)(2,1)S(1)}, bf16[128,512]{1,0:T(8,128)(2,1)S(1)}, u32[]{:S(2)}, u32[]{:S(2)}) collective-permute-start(bf16[128,512]{1,0:T(8,128)(2,1)S(1)} %convolution_convert_fusion.6), channel_id=1, source_target_pairs={{4,0},{8,4},{12,8},{16,12},{20,16},{24,20},{28,24},{5,1},{9,5},{13... | collective-permute-start | bytes 393224 | tf_op jit(solution)/shard_map/while/body/eval_jaxpr/ppermute | solution.py:14
  236.3 7.2 %collective-permute-start.1 = (bf16[128,512]{1,0:T(8,128)(2,1)S(1)}, bf16[128,512]{1,0:T(8,128)(2,1)S(1)}, u32[]{:S(2)}, u32[]{:S(2)}) collective-permute-start(bf16[128,512]{1,0:T(8,128)(2,1)S(1)} %convolution_convert_fusion.6), channel_id=1, source_target_pairs={{4,0},{8,4},{12,8},{16,12},{20,16},{24,20},{28,24},{5,1},{9,5},{13... | collective-permute-start | bytes 393224 | tf_op jit(solution)/shard_map/while/body/eval_jaxpr/ppermute | solution.py:14
  244.3 7.2 %collective-permute-start.1 = (bf16[128,512]{1,0:T(8,128)(2,1)S(1)}, bf16[128,512]{1,0:T(8,128)(2,1)S(1)}, u32[]{:S(2)}, u32[]{:S(2)}) collective-permute-start(bf16[128,512]{1,0:T(8,128)(2,1)S(1)} %convolution_convert_fusion.6), channel_id=1, source_target_pairs={{4,0},{8,4},{12,8},{16,12},{20,16},{24,20},{28,24},{5,1},{9,5},{13... | collective-permute-start | bytes 393224 | tf_op jit(solution)/shard_map/while/body/eval_jaxpr/ppermute | solution.py:14
  252.2 7.2 %collective-permute-start.1 = (bf16[128,512]{1,0:T(8,128)(2,1)S(1)}, bf16[128,512]{1,0:T(8,128)(2,1)S(1)}, u32[]{:S(2)}, u32[]{:S(2)}) collective-permute-start(bf16[128,512]{1,0:T(8,128)(2,1)S(1)} %convolution_convert_fusion.6), channel_id=1, source_target_pairs={{4,0},{8,4},{12,8},{16,12},{20,16},{24,20},{28,24},{5,1},{9,5},{13... | collective-permute-start | bytes 393224 | tf_op jit(solution)/shard_map/while/body/eval_jaxpr/ppermute | solution.py:14
  260.2 7.2 %collective-permute-start.1 = (bf16[128,512]{1,0:T(8,128)(2,1)S(1)}, bf16[128,512]{1,0:T(8,128)(2,1)S(1)}, u32[]{:S(2)}, u32[]{:S(2)}) collective-permute-start(bf16[128,512]{1,0:T(8,128)(2,1)S(1)} %convolution_convert_fusion.6), channel_id=1, source_target_pairs={{4,0},{8,4},{12,8},{16,12},{20,16},{24,20},{28,24},{5,1},{9,5},{13... | collective-permute-start | bytes 393224 | tf_op jit(solution)/shard_map/while/body/eval_jaxpr/ppermute | solution.py:14
  268.2 7.2 %collective-permute-start.1 = (bf16[128,512]{1,0:T(8,128)(2,1)S(1)}, bf16[128,512]{1,0:T(8,128)(2,1)S(1)}, u32[]{:S(2)}, u32[]{:S(2)}) collective-permute-start(bf16[128,512]{1,0:T(8,128)(2,1)S(1)} %convolution_convert_fusion.6), channel_id=1, source_target_pairs={{4,0},{8,4},{12,8},{16,12},{20,16},{24,20},{28,24},{5,1},{9,5},{13... | collective-permute-start | bytes 393224 | tf_op jit(solution)/shard_map/while/body/eval_jaxpr/ppermute | solution.py:14
  276.1 7.2 %collective-permute-start.1 = (bf16[128,512]{1,0:T(8,128)(2,1)S(1)}, bf16[128,512]{1,0:T(8,128)(2,1)S(1)}, u32[]{:S(2)}, u32[]{:S(2)}) collective-permute-start(bf16[128,512]{1,0:T(8,128)(2,1)S(1)} %convolution_convert_fusion.6), channel_id=1, source_target_pairs={{4,0},{8,4},{12,8},{16,12},{20,16},{24,20},{28,24},{5,1},{9,5},{13... | collective-permute-start | bytes 393224 | tf_op jit(solution)/shard_map/while/body/eval_jaxpr/ppermute | solution.py:14
  289.0 137.8 %all-gather.3.cloned.1.call-start = ((), (), s32[]{:S(2)}) async-start(), calls=%async_computation.3 | async-start | bytes 5242880 | tf_op jit(solution)/shard_map/all_gather | solution.py:131
  296.1 11.5 %all-to-all-start = ((bf16[2,128,512]{1,0,2:T(2,128)(2,1)}), bf16[2,128,512]{1,0,2:T(2,128)(2,1)}, u32[]{:S(2)}, u32[]{:S(2)}) async-start(bf16[2,128,512]{1,0,2:T(2,128)(2,1)} %copy.10), calls=%async_computation | async-start | bytes 524288 | tf_op jit(solution)/shard_map/all_to_all | solution.py:127
  307.6 42.5 %all-to-all-start.1 = ((bf16[2,128,2048]{1,0,2:T(2,128)(2,1)}), bf16[2,128,2048]{1,0,2:T(2,128)(2,1)S(1)}, u32[]{:S(2)}, u32[]{:S(2)}) async-start(bf16[2,128,2048]{1,0,2:T(2,128)(2,1)} %copy.13), calls=%async_computation.1 | async-start | bytes 2097152 | tf_op jit(solution)/shard_map/all_to_all | solution.py:128
  (19 other events, 170.4 us)
Sparse Core Ops, SparseCore 0:
  11.6 56.1 all-reduce.1
  289.1 52.3 all-gather.4
  343.7 83.0 all-gather.2
where the time goes:
time: 439 us; the launch traced here: 438 us
  waiting for transfers between devices  237 us (54%)
  matrix products  86.1 us (20%)
  starting transfers between devices  74.1 us (17%)
  between operations  14.2 us (3%)
  local copies, waits for them, and re-layouts  13.4 us (3%)
  other arithmetic  12.5 us (3%)
    all_gather x1, waiting for transfers between devices, shards(): lax.all_gather(delta_all, 'dp', axis=1, tiled=True)  72 us
    ppermute x22, starting transfers between devices, shifted(): return lax.ppermute(block, axis, route)  65.9 us
    ppermute x22, waiting for transfers between devices, shifted(): return lax.ppermute(block, axis, route)  65.8 us
    psum x1, waiting for transfers between devices, shards(): start = lax.psum(picked.astype(jnp.bfloat16), 'depth').astype(jnp.float32)  57.6 us
    all_to_all x1, waiting for transfers between devices, shards(): lax.all_to_all(hidden_all, 'dp', split_axis=2, concat_axis=1, tiled=True)  37 us
    dot_general x7, matrix products, layer_adjoint(): lax.dot_general(delta, weight_up, (((1,), (1,)), ((), ())), preferred_ele...  26.4 us
    dot_general x7, matrix products, layer_forward(): jnp.dot(hidden, weight_down, preferred_element_type=jnp.float32)  21.2 us
  transfers between devices with their start and end apart: 27, of which 22 were waited for; matrix products, arithmetic and copies ran while one was open for 9% of the time, Pallas kernels for 0%

commit v1 on v0

--- a/solution.py
+++ b/solution.py
@@ -6,6 +6,13 @@
 RELAX = 3
 EPSILON = 1e-06
 GAMMA = 0.05
+
+
+def swap_blocks(shard, axis, split, join):
+    size = lax.axis_size(axis)
+    shards = jnp.stack(jnp.split(shard, size, axis=split), axis=0)
+    shards = lax.all_to_all(shards, axis, split_axis=0, concat_axis=0)
+    return jnp.concatenate(shards, axis=join)
 
 
 def shifted(block, axis, distance):
@@ -125,7 +132,7 @@
     low_all = jnp.stack(lows, 0)
     normed_part, hidden_part = (
         lax.all_to_all(normed_all, "dp", split_axis=2, concat_axis=1, tiled=True),
-        lax.all_to_all(hidden_all, "dp", split_axis=2, concat_axis=1, tiled=True),
+        swap_blocks(hidden_all, "dp", 2, 1),
     )
     delta_whole, low_whole = (
         lax.all_gather(delta_all, "dp", axis=1, tiled=True),

time: 439 us -> 440 us (level)
  local copies, waits for them, and re-layouts: 13.4 us -> 8.3 us
  waiting for transfers between devices: 237 us -> 242 us
  transfers between devices with their start and end apart: 27 -> 27, of which waited for: 22 -> 22; matrix products, arithmetic and copies ran while one was open for 9% -> 8% of each run, Pallas kernels for 0% -> 0%
where the time goes in v1:
time: 440 us; the launch traced here: 439 us
  waiting for transfers between devices  242 us (55%)
  matrix products  86.7 us (20%)
  starting transfers between devices  74.2 us (17%)
  between operations  14.2 us (3%)
  other arithmetic  13 us (3%)
  local copies, waits for them, and re-layouts  8.3 us (2%)
    all_gather x1, waiting for transfers between devices, shards(): lax.all_gather(delta_all, 'dp', axis=1, tiled=True)  75.2 us
    ppermute x22, starting transfers between devices, shifted(): return lax.ppermute(block, axis, route)  65.9 us
    ppermute x22, waiting for transfers between devices, shifted(): return lax.ppermute(block, axis, route)  65.7 us
    psum x1, waiting for transfers between devices, shards(): start = lax.psum(picked.astype(jnp.bfloat16), 'depth').astype(jnp.float32)  57.6 us
    all_to_all x1, waiting for transfers between devices, swap_blocks(): shards = lax.all_to_all(shards, axis, split_axis=0, concat_axis=0)  39.5 us
    dot_general x7, matrix products, layer_adjoint(): lax.dot_general(delta, weight_up, (((1,), (1,)), ((), ())), preferred_ele...  27.1 us
    dot_general x7, matrix products, layer_forward(): jnp.dot(hidden, weight_down, preferred_element_type=jnp.float32)  21.2 us
  transfers between devices with their start and end apart: 27, of which 22 were waited for; matrix products, arithmetic and copies ran while one was open for 8% of the time, Pallas kernels for 0%

profile of v1, /device:TPU:0, one launch (start us, length us, event | category | flops | bytes accessed | tf_op | source)
XLA Modules:
  0.0 438.7 jit_solution(4182290960799304382)
XLA Ops:
  10.2 57.6 %all-reduce.2.cloned.1.call-done = bf16[128,512]{1,0:T(8,128)(2,1)} async-done(((bf16[128,512]{1,0:T(8,128)(2,1)}), bf16[128,512]{1,0:T(8,128)(2,1)}) %all-reduce.2.cloned.1.call-update) | async-done | bytes 131088 | tf_op jit(solution)/shard_map/psum | solution.py:66
  114.8 50.3 %while.22 = (s32[]{:T(128)}, f32[128,512]{1,0:T(8,128)S(1)}, f32[128,512]{1,0:T(8,128)S(1)}, f32[512,512]{1,0:T(8,128)S(1)}, s32[]{:T(128)}, /*index=5*/s32[]{:T(128)}) while((s32[]{:T(128)}, f32[128,512]{1,0:T(8,128)S(1)}, f32[128,512]{1,0:T(8,128)S(1)}, f32[512,512]{1,0:T(8,128)S(1)}, s32[]{:T(128)}, /*index=5*/s32[]{:T(128)}) %tuple.68), condition=%wide.region_8.9_spmd.clone, body=%wide.region_7.8_spmd.clone.sunk | while | flops 402915328 | bytes 2621559 | solution.py:85
  115.6 5.4 %collective-permute-start = (bf16[128,512]{1,0:T(8,128)(2,1)S(1)}, bf16[128,512]{1,0:T(8,128)(2,1)S(1)}, u32[]{:S(2)}, u32[]{:S(2)}) collective-permute-start(bf16[128,512]{1,0:T(8,128)(2,1)S(1)} %convolution_convert_fusion.5), channel_id=1, source_target_pairs={{0,4},{4,8},{8,12},{12,16},{16,20},{20,24},{24,28},{1,5},{5,9},{9,... | collective-permute-start | bytes 393224 | tf_op jit(solution)/shard_map/while/body/eval_jaxpr/ppermute | solution.py:21
  122.8 5.2 %collective-permute-start = (bf16[128,512]{1,0:T(8,128)(2,1)S(1)}, bf16[128,512]{1,0:T(8,128)(2,1)S(1)}, u32[]{:S(2)}, u32[]{:S(2)}) collective-permute-start(bf16[128,512]{1,0:T(8,128)(2,1)S(1)} %convolution_convert_fusion.5), channel_id=1, source_target_pairs={{0,4},{4,8},{8,12},{12,16},{16,20},{20,24},{24,28},{1,5},{5,9},{9,... | collective-permute-start | bytes 393224 | tf_op jit(solution)/shard_map/while/body/eval_jaxpr/ppermute | solution.py:21
  129.8 5.3 %collective-permute-start = (bf16[128,512]{1,0:T(8,128)(2,1)S(1)}, bf16[128,512]{1,0:T(8,128)(2,1)S(1)}, u32[]{:S(2)}, u32[]{:S(2)}) collective-permute-start(bf16[128,512]{1,0:T(8,128)(2,1)S(1)} %convolution_convert_fusion.5), channel_id=1, source_target_pairs={{0,4},{4,8},{8,12},{12,16},{16,20},{20,24},{24,28},{1,5},{5,9},{9,... | collective-permute-start | bytes 393224 | tf_op jit(solution)/shard_map/while/body/eval_jaxpr/ppermute | solution.py:21
  136.8 5.3 %collective-permute-start = (bf16[128,512]{1,0:T(8,128)(2,1)S(1)}, bf16[128,512]{1,0:T(8,128)(2,1)S(1)}, u32[]{:S(2)}, u32[]{:S(2)}) collective-permute-start(bf16[128,512]{1,0:T(8,128)(2,1)S(1)} %convolution_convert_fusion.5), channel_id=1, source_target_pairs={{0,4},{4,8},{8,12},{12,16},{16,20},{20,24},{24,28},{1,5},{5,9},{9,... | collective-permute-start | bytes 393224 | tf_op jit(solution)/shard_map/while/body/eval_jaxpr/ppermute | solution.py:21
  143.9 5.3 %collective-permute-start = (bf16[128,512]{1,0:T(8,128)(2,1)S(1)}, bf16[128,512]{1,0:T(8,128)(2,1)S(1)}, u32[]{:S(2)}, u32[]{:S(2)}) collective-permute-start(bf16[128,512]{1,0:T(8,128)(2,1)S(1)} %convolution_convert_fusion.5), channel_id=1, source_target_pairs={{0,4},{4,8},{8,12},{12,16},{16,20},{20,24},{24,28},{1,5},{5,9},{9,... | collective-permute-start | bytes 393224 | tf_op jit(solution)/shard_map/while/body/eval_jaxpr/ppermute | solution.py:21
  151.0 5.3 %collective-permute-start = (bf16[128,512]{1,0:T(8,128)(2,1)S(1)}, bf16[128,512]{1,0:T(8,128)(2,1)S(1)}, u32[]{:S(2)}, u32[]{:S(2)}) collective-permute-start(bf16[128,512]{1,0:T(8,128)(2,1)S(1)} %convolution_convert_fusion.5), channel_id=1, source_target_pairs={{0,4},{4,8},{8,12},{12,16},{16,20},{20,24},{24,28},{1,5},{5,9},{9,... | collective-permute-start | bytes 393224 | tf_op jit(solution)/shard_map/while/body/eval_jaxpr/ppermute | solution.py:21
  158.0 6.2 %collective-permute-start = (bf16[128,512]{1,0:T(8,128)(2,1)S(1)}, bf16[128,512]{1,0:T(8,128)(2,1)S(1)}, u32[]{:S(2)}, u32[]{:S(2)}) collective-permute-start(bf16[128,512]{1,0:T(8,128)(2,1)S(1)} %convolution_convert_fusion.5), channel_id=1, source_target_pairs={{0,4},{4,8},{8,12},{12,16},{16,20},{20,24},{24,28},{1,5},{5,9},{9,... | collective-permute-start | bytes 393224 | tf_op jit(solution)/shard_map/while/body/eval_jaxpr/ppermute | solution.py:21
  181.6 5.7 %collective-permute-done.6 = bf16[128,512]{1,0:T(8,128)(2,1)S(1)} collective-permute-done((bf16[128,512]{1,0:T(8,128)(2,1)S(1)}, bf16[128,512]{1,0:T(8,128)(2,1)S(1)}, u32[]{:S(2)}, u32[]{:S(2)}) %collective-permute-start.6) | collective-permute-done | bytes 131104 | tf_op jit(solution)/shard_map/ppermute | solution.py:21
  197.4 6.6 %collective-permute-done.7 = bf16[128,512]{1,0:T(8,128)(2,1)S(1)} collective-permute-done((bf16[128,512]{1,0:T(8,128)(2,1)S(1)}, bf16[128,512]{1,0:T(8,128)(2,1)S(1)}, u32[]{:S(2)}, u32[]{:S(2)}) %collective-permute-start.7) | collective-permute-done | bytes 131104 | tf_op jit(solution)/shard_map/ppermute | solution.py:21
  207.1 4.8 %multiply_reduce_fusion.2 = (f32[128]{0:T(128)S(1)}, f32[128,512]{1,0:T(8,128)}) fusion(f32[128,512]{1,0:T(8,128)S(1)} %get-tuple-element.130, f32[128]{0:T(128)S(1)} %add_rsqrt_fusion, bf16[2,512,2048]{2,1,0:T(8,128)(2,1)} %param.11, f32[128,2048]{1,0:T(8,128)} %fusion.43, bf16[2,2048,512]{2,1,0:T(8,128)(2,1)} %param.12, ...), kind=kOutput, calls=%fused_computation.186 | convolution fusion | flops 539688832 | bytes 6030337 | tf_op jit(solution)/shard_map/dot_general | solution.py:41
  213.0 4.8 %multiply_reduce_fusion.1 = (f32[128]{0:T(128)S(1)}, f32[128,512]{1,0:T(8,128)}) fusion(f32[128,512]{1,0:T(8,128)S(1)} %get-tuple-element.109, f32[128]{0:T(128)S(1)} %add_rsqrt_fusion.1, bf16[2,512,2048]{2,1,0:T(8,128)(2,1)} %param.11, f32[128,2048]{1,0:T(8,128)} %copy-done.3, f32[128,512]{1,0:T(8,128)S(1)} %multiply_add_fusion.8, ...), kind=kOutput, calls=%fused_computation.184 | convolution fusion | flops 539492224 | bytes 6030336 | tf_op jit(solution)/shard_map/dot_general | solution.py:41
  227.8 56.4 %while.23 = (s32[]{:T(128)}, f32[128,512]{1,0:T(8,128)S(1)}, f32[128,512]{1,0:T(8,128)S(1)}, f32[512,512]{1,0:T(8,128)S(1)}, s32[]{:T(128)}, /*index=5*/s32[]{:T(128)}) while((s32[]{:T(128)}, f32[128,512]{1,0:T(8,128)S(1)}, f32[128,512]{1,0:T(8,128)S(1)}, f32[512,512]{1,0:T(8,128)S(1)}, s32[]{:T(128)}, ...), condition=%wide.region_18.19_spmd.clone, body=%wide.region_17.18_spmd.clone.sunk | while | flops 402915328 | bytes 2621559 | solution.py:119
  229.9 6.6 %collective-permute-done.1 = bf16[128,512]{1,0:T(8,128)(2,1)S(1)} collective-permute-done((bf16[128,512]{1,0:T(8,128)(2,1)S(1)}, bf16[128,512]{1,0:T(8,128)(2,1)S(1)}, u32[]{:S(2)}, u32[]{:S(2)}) %collective-permute-start.1) | collective-permute-done | bytes 131104 | tf_op jit(solution)/shard_map/while/body/eval_jaxpr/ppermute | solution.py:21
  238.5 5.9 %collective-permute-done.1 = bf16[128,512]{1,0:T(8,128)(2,1)S(1)} collective-permute-done((bf16[128,512]{1,0:T(8,128)(2,1)S(1)}, bf16[128,512]{1,0:T(8,128)(2,1)S(1)}, u32[]{:S(2)}, u32[]{:S(2)}) %collective-permute-start.1) | collective-permute-done | bytes 131104 | tf_op jit(solution)/shard_map/while/body/eval_jaxpr/ppermute | solution.py:21
  246.5 5.9 %collective-permute-done.1 = bf16[128,512]{1,0:T(8,128)(2,1)S(1)} collective-permute-done((bf16[128,512]{1,0:T(8,128)(2,1)S(1)}, bf16[128,512]{1,0:T(8,128)(2,1)S(1)}, u32[]{:S(2)}, u32[]{:S(2)}) %collective-permute-start.1) | collective-permute-done | bytes 131104 | tf_op jit(solution)/shard_map/while/body/eval_jaxpr/ppermute | solution.py:21
  254.4 5.9 %collective-permute-done.1 = bf16[128,512]{1,0:T(8,128)(2,1)S(1)} collective-permute-done((bf16[128,512]{1,0:T(8,128)(2,1)S(1)}, bf16[128,512]{1,0:T(8,128)(2,1)S(1)}, u32[]{:S(2)}, u32[]{:S(2)}) %collective-permute-start.1) | collective-permute-done | bytes 131104 | tf_op jit(solution)/shard_map/while/body/eval_jaxpr/ppermute | solution.py:21
  262.4 5.9 %collective-permute-done.1 = bf16[128,512]{1,0:T(8,128)(2,1)S(1)} collective-permute-done((bf16[128,512]{1,0:T(8,128)(2,1)S(1)}, bf16[128,512]{1,0:T(8,128)(2,1)S(1)}, u32[]{:S(2)}, u32[]{:S(2)}) %collective-permute-start.1) | collective-permute-done | bytes 131104 | tf_op jit(solution)/shard_map/while/body/eval_jaxpr/ppermute | solution.py:21
  270.4 5.9 %collective-permute-done.1 = bf16[128,512]{1,0:T(8,128)(2,1)S(1)} collective-permute-done((bf16[128,512]{1,0:T(8,128)(2,1)S(1)}, bf16[128,512]{1,0:T(8,128)(2,1)S(1)}, u32[]{:S(2)}, u32[]{:S(2)}) %collective-permute-start.1) | collective-permute-done | bytes 131104 | tf_op jit(solution)/shard_map/while/body/eval_jaxpr/ppermute | solution.py:21
  278.3 5.9 %collective-permute-done.1 = bf16[128,512]{1,0:T(8,128)(2,1)S(1)} collective-permute-done((bf16[128,512]{1,0:T(8,128)(2,1)S(1)}, bf16[128,512]{1,0:T(8,128)(2,1)S(1)}, u32[]{:S(2)}, u32[]{:S(2)}) %collective-permute-start.1) | collective-permute-done | bytes 131104 | tf_op jit(solution)/shard_map/while/body/eval_jaxpr/ppermute | solution.py:21
  293.9 4.6 %all-to-all-start = ((bf16[2,128,512]{1,0,2:T(2,128)(2,1)}), bf16[2,128,512]{1,0,2:T(2,128)(2,1)S(1)}, u32[]{:S(2)}, u32[]{:S(2)}) async-start(bf16[2,128,512]{1,0,2:T(2,128)(2,1)} %copy.13), calls=%async_computation | async-start | bytes 524288 | tf_op jit(solution)/shard_map/all_to_all | solution.py:134
  309.8 39.5 %all-to-all-done.1 = bf16[4,2,128,512]{3,2,1,0:T(8,128)(2,1)S(1)} async-done(((bf16[4,2,128,512]{3,2,1,0:T(8,128)(2,1)}), bf16[4,2,128,512]{3,2,1,0:T(8,128)(2,1)S(1)}, u32[]{:S(2)}, u32[]{:S(2)}) %all-to-all-start.1) | async-done | bytes 1048608 | tf_op jit(solution)/shard_map/all_to_all | solution.py:14
  352.8 75.2 %all-gather.3.cloned.1.call-done = bf16[2,512,2048]{2,1,0:T(8,128)(2,1)} async-done(((bf16[2,128,2048]{2,1,0:T(8,128)(2,1)}), bf16[2,512,2048]{2,1,0:T(8,128)(2,1)}) %all-gather.3.cloned.1.call-update) | async-done | bytes 4194320 | tf_op jit(solution)/shard_map/all_gather | solution.py:138
  (161 shorter events, 145.2 us)
Async XLA Ops:
  7.2 60.6 %all-reduce.2.cloned.1.call-start = ((), (), s32[]{:S(2)}) async-start(), calls=%async_computation.2 | async-start | bytes 262144 | tf_op jit(solution)/shard_map/psum | solution.py:66
  10.1 339.3 %all-gather.5.cloned.1.call-start = ((), (), s32[]{:S(2)}) async-start(), calls=%async_computation.4 | async-start | bytes 1310720 | tf_op jit(solution)/shard_map/all_gather | solution.py:139
  87.8 7.2 %collective-permute-start.3 = (f32[128,512]{1,0:T(8,128)}, f32[128,512]{1,0:T(8,128)S(1)}, u32[]{:S(2)}, u32[]{:S(2)}) collective-permute-start(f32[128,512]{1,0:T(8,128)} %fusion.118), channel_id=1, source_target_pairs={{0,4},{4,8},{8,12},{12,16},{16,20},{20,24},{24,28},{1,5},{5,9},{9,... | collective-permute-start | bytes 786440 | tf_op jit(solution)/shard_map/ppermute | solution.py:21
  103.6 10.0 %collective-permute-start.4 = (f32[128,512]{1,0:T(8,128)}, f32[128,512]{1,0:T(8,128)}, u32[]{:S(2)}, u32[]{:S(2)}) collective-permute-start(f32[128,512]{1,0:T(8,128)} %fusion.121), channel_id=1, source_target_pairs={{0,4},{4,8},{8,12},{12,16},{16,20},{20,24},{24,28},{1,5},{5,9},{9,... | collective-permute-start | bytes 786440 | tf_op jit(solution)/shard_map/ppermute | solution.py:21
  115.6 6.4 %collective-permute-start = (bf16[128,512]{1,0:T(8,128)(2,1)S(1)}, bf16[128,512]{1,0:T(8,128)(2,1)S(1)}, u32[]{:S(2)}, u32[]{:S(2)}) collective-permute-start(bf16[128,512]{1,0:T(8,128)(2,1)S(1)} %convolution_convert_fusion.5), channel_id=1, source_target_pairs={{0,4},{4,8},{8,12},{12,16},{16,20},{20,24},{24,28},{1,5},{5,9},{9,... | collective-permute-start | bytes 393224 | tf_op jit(solution)/shard_map/while/body/eval_jaxpr/ppermute | solution.py:21
  129.8 6.3 %collective-permute-start = (bf16[128,512]{1,0:T(8,128)(2,1)S(1)}, bf16[128,512]{1,0:T(8,128)(2,1)S(1)}, u32[]{:S(2)}, u32[]{:S(2)}) collective-permute-start(bf16[128,512]{1,0:T(8,128)(2,1)S(1)} %convolution_convert_fusion.5), channel_id=1, source_target_pairs={{0,4},{4,8},{8,12},{12,16},{16,20},{20,24},{24,28},{1,5},{5,9},{9,... | collective-permute-start | bytes 393224 | tf_op jit(solution)/shard_map/while/body/eval_jaxpr/ppermute | solution.py:21
  136.8 6.3 %collective-permute-start = (bf16[128,512]{1,0:T(8,128)(2,1)S(1)}, bf16[128,512]{1,0:T(8,128)(2,1)S(1)}, u32[]{:S(2)}, u32[]{:S(2)}) collective-permute-start(bf16[128,512]{1,0:T(8,128)(2,1)S(1)} %convolution_convert_fusion.5), channel_id=1, source_target_pairs={{0,4},{4,8},{8,12},{12,16},{16,20},{20,24},{24,28},{1,5},{5,9},{9,... | collective-permute-start | bytes 393224 | tf_op jit(solution)/shard_map/while/body/eval_jaxpr/ppermute | solution.py:21
  143.9 6.3 %collective-permute-start = (bf16[128,512]{1,0:T(8,128)(2,1)S(1)}, bf16[128,512]{1,0:T(8,128)(2,1)S(1)}, u32[]{:S(2)}, u32[]{:S(2)}) collective-permute-start(bf16[128,512]{1,0:T(8,128)(2,1)S(1)} %convolution_convert_fusion.5), channel_id=1, source_target_pairs={{0,4},{4,8},{8,12},{12,16},{16,20},{20,24},{24,28},{1,5},{5,9},{9,... | collective-permute-start | bytes 393224 | tf_op jit(solution)/shard_map/while/body/eval_jaxpr/ppermute | solution.py:21
  151.0 6.3 %collective-permute-start = (bf16[128,512]{1,0:T(8,128)(2,1)S(1)}, bf16[128,512]{1,0:T(8,128)(2,1)S(1)}, u32[]{:S(2)}, u32[]{:S(2)}) collective-permute-start(bf16[128,512]{1,0:T(8,128)(2,1)S(1)} %convolution_convert_fusion.5), channel_id=1, source_target_pairs={{0,4},{4,8},{8,12},{12,16},{16,20},{20,24},{24,28},{1,5},{5,9},{9,... | collective-permute-start | bytes 393224 | tf_op jit(solution)/shard_map/while/body/eval_jaxpr/ppermute | solution.py:21
  158.0 7.1 %collective-permute-start = (bf16[128,512]{1,0:T(8,128)(2,1)S(1)}, bf16[128,512]{1,0:T(8,128)(2,1)S(1)}, u32[]{:S(2)}, u32[]{:S(2)}) collective-permute-start(bf16[128,512]{1,0:T(8,128)(2,1)S(1)} %convolution_convert_fusion.5), channel_id=1, source_target_pairs={{0,4},{4,8},{8,12},{12,16},{16,20},{20,24},{24,28},{1,5},{5,9},{9,... | collective-permute-start | bytes 393224 | tf_op jit(solution)/shard_map/while/body/eval_jaxpr/ppermute | solution.py:21
  180.3 7.0 %collective-permute-start.6 = (bf16[128,512]{1,0:T(8,128)(2,1)S(1)}, bf16[128,512]{1,0:T(8,128)(2,1)S(1)}, u32[]{:S(2)}, u32[]{:S(2)}) collective-permute-start(bf16[128,512]{1,0:T(8,128)(2,1)S(1)} %add_convert_fusion.3), channel_id=1, source_target_pairs={{4,0},{8,4},{12,8},{16,12},{20,16},{24,20},{28,24},{5,1},{9,5},{13... | collective-permute-start | bytes 393224 | tf_op jit(solution)/shard_map/ppermute | solution.py:21
  196.1 7.9 %collective-permute-start.7 = (bf16[128,512]{1,0:T(8,128)(2,1)S(1)}, bf16[128,512]{1,0:T(8,128)(2,1)S(1)}, u32[]{:S(2)}, u32[]{:S(2)}) collective-permute-start(bf16[128,512]{1,0:T(8,128)(2,1)S(1)} %add_convert_fusion.2), channel_id=1, source_target_pairs={{4,0},{8,4},{12,8},{16,12},{20,16},{24,20},{28,24},{5,1},{9,5},{13... | collective-permute-start | bytes 393224 | tf_op jit(solution)/shard_map/ppermute | solution.py:21
  205.8 17.3 %collective-permute-start.9 = (bf16[128,512]{1,0:T(8,128)(2,1)}, bf16[128,512]{1,0:T(8,128)(2,1)}, u32[]{:S(2)}, u32[]{:S(2)}) collective-permute-start(bf16[128,512]{1,0:T(8,128)(2,1)} %convolution_convert_fusion.2), channel_id=1, source_target_pairs={{4,0},{8,4},{12,8},{16,12},{20,16},{24,20},{28,24},{5,1},{9,5},{13... | collective-permute-start | bytes 393224 | tf_op jit(solution)/shard_map/ppermute | solution.py:21
  219.0 7.8 %collective-permute-start.8 = (bf16[128,512]{1,0:T(8,128)(2,1)S(1)}, bf16[128,512]{1,0:T(8,128)(2,1)}, u32[]{:S(2)}, u32[]{:S(2)}) collective-permute-start(bf16[128,512]{1,0:T(8,128)(2,1)S(1)} %get-tuple-element.118), channel_id=1, source_target_pairs={{4,0},{8,4},{12,8},{16,12},{20,16},{24,20},{28,24},{5,1},{9,5},{13... | collective-permute-start | bytes 393224 | tf_op jit(solution)/shard_map/ppermute | solution.py:21
  228.6 7.9 %collective-permute-start.1 = (bf16[128,512]{1,0:T(8,128)(2,1)S(1)}, bf16[128,512]{1,0:T(8,128)(2,1)S(1)}, u32[]{:S(2)}, u32[]{:S(2)}) collective-permute-start(bf16[128,512]{1,0:T(8,128)(2,1)S(1)} %convolution_convert_fusion.6), channel_id=1, source_target_pairs={{4,0},{8,4},{12,8},{16,12},{20,16},{24,20},{28,24},{5,1},{9,5},{13... | collective-permute-start | bytes 393224 | tf_op jit(solution)/shard_map/while/body/eval_jaxpr/ppermute | solution.py:21
  237.2 7.2 %collective-permute-start.1 = (bf16[128,512]{1,0:T(8,128)(2,1)S(1)}, bf16[128,512]{1,0:T(8,128)(2,1)S(1)}, u32[]{:S(2)}, u32[]{:S(2)}) collective-permute-start(bf16[128,512]{1,0:T(8,128)(2,1)S(1)} %convolution_convert_fusion.6), channel_id=1, source_target_pairs={{4,0},{8,4},{12,8},{16,12},{20,16},{24,20},{28,24},{5,1},{9,5},{13... | collective-permute-start | bytes 393224 | tf_op jit(solution)/shard_map/while/body/eval_jaxpr/ppermute | solution.py:21
  245.2 7.2 %collective-permute-start.1 = (bf16[128,512]{1,0:T(8,128)(2,1)S(1)}, bf16[128,512]{1,0:T(8,128)(2,1)S(1)}, u32[]{:S(2)}, u32[]{:S(2)}) collective-permute-start(bf16[128,512]{1,0:T(8,128)(2,1)S(1)} %convolution_convert_fusion.6), channel_id=1, source_target_pairs={{4,0},{8,4},{12,8},{16,12},{20,16},{24,20},{28,24},{5,1},{9,5},{13... | collective-permute-start | bytes 393224 | tf_op jit(solution)/shard_map/while/body/eval_jaxpr/ppermute | solution.py:21
  253.1 7.2 %collective-permute-start.1 = (bf16[128,512]{1,0:T(8,128)(2,1)S(1)}, bf16[128,512]{1,0:T(8,128)(2,1)S(1)}, u32[]{:S(2)}, u32[]{:S(2)}) collective-permute-start(bf16[128,512]{1,0:T(8,128)(2,1)S(1)} %convolution_convert_fusion.6), channel_id=1, source_target_pairs={{4,0},{8,4},{12,8},{16,12},{20,16},{24,20},{28,24},{5,1},{9,5},{13... | collective-permute-start | bytes 393224 | tf_op jit(solution)/shard_map/while/body/eval_jaxpr/ppermute | solution.py:21
  261.1 7.2 %collective-permute-start.1 = (bf16[128,512]{1,0:T(8,128)(2,1)S(1)}, bf16[128,512]{1,0:T(8,128)(2,1)S(1)}, u32[]{:S(2)}, u32[]{:S(2)}) collective-permute-start(bf16[128,512]{1,0:T(8,128)(2,1)S(1)} %convolution_convert_fusion.6), channel_id=1, source_target_pairs={{4,0},{8,4},{12,8},{16,12},{20,16},{24,20},{28,24},{5,1},{9,5},{13... | collective-permute-start | bytes 393224 | tf_op jit(solution)/shard_map/while/body/eval_jaxpr/ppermute | solution.py:21
  269.1 7.2 %collective-permute-start.1 = (bf16[128,512]{1,0:T(8,128)(2,1)S(1)}, bf16[128,512]{1,0:T(8,128)(2,1)S(1)}, u32[]{:S(2)}, u32[]{:S(2)}) collective-permute-start(bf16[128,512]{1,0:T(8,128)(2,1)S(1)} %convolution_convert_fusion.6), channel_id=1, source_target_pairs={{4,0},{8,4},{12,8},{16,12},{20,16},{24,20},{28,24},{5,1},{9,5},{13... | collective-permute-start | bytes 393224 | tf_op jit(solution)/shard_map/while/body/eval_jaxpr/ppermute | solution.py:21
  277.0 7.2 %collective-permute-start.1 = (bf16[128,512]{1,0:T(8,128)(2,1)S(1)}, bf16[128,512]{1,0:T(8,128)(2,1)S(1)}, u32[]{:S(2)}, u32[]{:S(2)}) collective-permute-start(bf16[128,512]{1,0:T(8,128)(2,1)S(1)} %convolution_convert_fusion.6), channel_id=1, source_target_pairs={{4,0},{8,4},{12,8},{16,12},{20,16},{24,20},{28,24},{5,1},{9,5},{13... | collective-permute-start | bytes 393224 | tf_op jit(solution)/shard_map/while/body/eval_jaxpr/ppermute | solution.py:21
  289.3 138.7 %all-gather.3.cloned.1.call-start = ((), (), s32[]{:S(2)}) async-start(), calls=%async_computation.3 | async-start | bytes 5242880 | tf_op jit(solution)/shard_map/all_gather | solution.py:138
  293.9 11.4 %all-to-all-start = ((bf16[2,128,512]{1,0,2:T(2,128)(2,1)}), bf16[2,128,512]{1,0,2:T(2,128)(2,1)S(1)}, u32[]{:S(2)}, u32[]{:S(2)}) async-start(bf16[2,128,512]{1,0,2:T(2,128)(2,1)} %copy.13), calls=%async_computation | async-start | bytes 524288 | tf_op jit(solution)/shard_map/all_to_all | solution.py:134
  305.3 44.1 %all-to-all-start.1 = ((bf16[4,2,128,512]{3,2,1,0:T(8,128)(2,1)}), bf16[4,2,128,512]{3,2,1,0:T(8,128)(2,1)S(1)}, u32[]{:S(2)}, u32[]{:S(2)}) async-start(bf16[4,2,128,512]{3,2,1,0:T(8,128)(2,1)} %pad_maximum_fusion.1), calls=%async_computation.1 | async-start | bytes 2097152 | tf_op jit(solution)/shard_map/all_to_all | solution.py:14
  (17 other events, 155.6 us)
Sparse Core Ops, SparseCore 0:
  11.6 56.1 all-reduce.1
  289.4 55.8 all-gather.4
  347.4 80.5 all-gather.2
